TPU v7x, 32 devices: a whole 2x2x4 slice. The times are simulated.
32 devices in a mesh: narrow: 4 (over z), wide: 8 (over y, x, core).
Axes of the slice: x: 2, y: 2, z: 4, core: 2. Of those that a mesh axis runs over, the one named last changes fastest.
Arguments:
- tokens: bfloat16 [12288, 640], P('wide'), may hold values from -6 to 6
- cotangent: bfloat16 [12288, 640], P('wide'), may hold values from -6 to 6
- seq_lens: int32 [8, 16], P('wide'), may hold values from 1 to 1024, 1536 in all within a row
- norm_gains: bfloat16 [2, 640], replicated, may hold values from 0.099609375 to 1.8984375
- norm_shifts: bfloat16 [2, 640], replicated, may hold values from -3 to 3
- w_qkv: bfloat16 [3, 640, 640], P(None, 'wide', 'narrow'), may hold values from -0.25 to 0.25
- w_attn_out: bfloat16 [640, 640], P('narrow', 'wide'), may hold values from -2 to 2
- w_ffn_in: bfloat16 [640, 5120], P('narrow', 'wide'), may hold values from -0.25 to 0.25
- w_ffn_down: bfloat16 [640, 5120], P('narrow', 'wide'), may hold values from -0.078125 to 0.078125
Outputs:
- layer_out: bfloat16 [12288, 640], P('wide')
- input_grad: bfloat16 [12288, 640], P('wide')
- grad_norm_gains: float32 [2, 640], P(None, 'wide')
- grad_norm_shifts: float32 [2, 640], P(None, 'wide')
- grad_qkv: float32 [3, 640, 640], P(None, 'wide', 'narrow')
- grad_attn_out: float32 [640, 640], P('narrow', 'wide')
- grad_ffn_in: float32 [640, 5120], P('narrow', 'wide')
- grad_ffn_down: float32 [640, 5120], P('narrow', 'wide')
Inputs may be any that keep to these rules, and one draw needn't show every extreme that they name: `seq_lens`: each row lists the lengths of the 16 sequences packed end to end in that index's 1536 slots; a row sums to 1536 and its largest entry is exactly 1024.
All inputs are finite; a program needn't handle non-finite values.
Results may differ from a plain program's by a relative error of at most 0.015.
Values may be sent and summed in bfloat16 or wider, within the bound.
No kernel may reach another device: no remote copies, remote signals or barrier semaphores. Data moves between devices by JAX's collectives and lax.ppermute only.
A program may use at most 128 MiB of HBM per device.

v0:
```python
from functools import partial
import jax
import jax.numpy as jnp
from jax import lax
from jax.sharding import PartitionSpec as P

HD = 32
QBLK = 512
FBLK = 128
EPS = 1e-05


def layer_norm(rows, gain, shift):
    center = rows - jnp.mean(rows, axis=-1, keepdims=True)
    spread = jnp.mean(center * center, axis=-1, keepdims=True)
    return center * lax.rsqrt(spread + EPS) * gain + shift


def segment_ids(lengths, count):
    ends = jnp.cumsum(lengths, dtype=jnp.int32)
    position = jnp.arange(count, dtype=jnp.int32)
    return jnp.sum((position[:, None] >= ends[None, :]).astype(jnp.int32), axis=1)


def block_scores(q_block, keys, seg_block, segment):
    scores = jnp.einsum("qd,kd->qk", q_block, keys, preferred_element_type=jnp.float32) * HD ** (
        -0.5
    )
    return jnp.where(seg_block[:, None] == segment[None, :], scores, -1e30)


def attend_forward(query, key, value, segment):
    count, width = query.shape
    starts = jnp.arange(count // QBLK, dtype=jnp.int32) * QBLK

    def one_head(head):
        q_head = lax.dynamic_slice_in_dim(query, head * HD, HD, 1)
        k_head = lax.dynamic_slice_in_dim(key, head * HD, HD, 1)
        v_head = lax.dynamic_slice_in_dim(value, head * HD, HD, 1)

        def one_block(start):
            q_block = lax.dynamic_slice_in_dim(q_head, start, QBLK, 0)
            seg_block = lax.dynamic_slice_in_dim(segment, start, QBLK, 0)
            scores = block_scores(q_block, k_head, seg_block, segment)
            top = jnp.max(scores, axis=1, keepdims=True)
            expd = jnp.exp(scores - top)
            total = jnp.sum(expd, axis=1, keepdims=True)
            weights = (expd / total).astype(jnp.bfloat16)
            result = jnp.dot(weights, v_head, preferred_element_type=jnp.float32)
            return (result, (top + jnp.log(total))[:, 0])

        results, logsum = lax.map(one_block, starts)
        return (results.reshape(count, HD), logsum.reshape(count))

    results, logsum = lax.map(one_head, jnp.arange(width // HD, dtype=jnp.int32))
    return (results.transpose(1, 0, 2).reshape(count, width), logsum)


def attend_backward(query, key, value, dattended, logsum, segment):
    count, width = query.shape
    starts = jnp.arange(count // QBLK, dtype=jnp.int32) * QBLK
    scale = HD ** (-0.5)

    def one_head(head):
        q_head = lax.dynamic_slice_in_dim(query, head * HD, HD, 1)
        k_head = lax.dynamic_slice_in_dim(key, head * HD, HD, 1)
        v_head = lax.dynamic_slice_in_dim(value, head * HD, HD, 1)
        d_head = lax.dynamic_slice_in_dim(dattended, head * HD, HD, 1)
        log_head = logsum[head]

        def one_block(carry, start):
            dkey, dvalue = carry
            q_block = lax.dynamic_slice_in_dim(q_head, start, QBLK, 0)
            d_block = lax.dynamic_slice_in_dim(d_head, start, QBLK, 0)
            seg_block = lax.dynamic_slice_in_dim(segment, start, QBLK, 0)
            log_block = lax.dynamic_slice_in_dim(log_head, start, QBLK, 0)
            scores = block_scores(q_block, k_head, seg_block, segment)
            prob = jnp.exp(scores - log_block[:, None])
            dprob = jnp.einsum("qd,kd->qk", d_block, v_head, preferred_element_type=jnp.float32)
            delta = jnp.sum(prob * dprob, axis=1, keepdims=True)
            dscore = (prob * (dprob - delta)).astype(jnp.bfloat16)
            dquery = jnp.dot(dscore, k_head, preferred_element_type=jnp.float32) * scale
            dkey = (
                dkey
                + jnp.einsum("qk,qd->kd", dscore, q_block, preferred_element_type=jnp.float32)
                * scale
            )
            dvalue = dvalue + jnp.einsum(
                "qk,qd->kd", prob.astype(jnp.bfloat16), d_block, preferred_element_type=jnp.float32
            )
            return ((dkey, dvalue), dquery)

        zeros = jnp.zeros((count, HD), jnp.float32)
        (dkey, dvalue), dquery = lax.scan(one_block, (zeros, zeros), starts)
        return (dquery.reshape(count, HD), dkey, dvalue)

    dquery, dkey, dvalue = lax.map(one_head, jnp.arange(width // HD, dtype=jnp.int32))

    def joined(arr):
        return arr.transpose(1, 0, 2).reshape(count, width)

    return (joined(dquery), joined(dkey), joined(dvalue))


def hidden_block(normed_mine, ffn_in_full, start):
    x_block = lax.dynamic_slice_in_dim(normed_mine, start, FBLK, 0)
    share = lax.psum_scatter(
        jnp.dot(x_block, ffn_in_full, preferred_element_type=jnp.float32),
        "narrow",
        scatter_dimension=0,
        tiled=True,
    )
    act_share = jax.nn.gelu(share, approximate=False).astype(jnp.bfloat16)
    act_rows = lax.all_gather(act_share, "narrow", axis=0, tiled=True)
    return (x_block, share, act_rows)


def local(
    tokens, cotangent, seq_lens, norm_gains, norm_shifts, w_qkv, w_attn_out, w_ffn_in, w_ffn_down
):
    count = tokens.shape[0]
    width = w_attn_out.shape[0]
    first_col = lax.axis_index("narrow") * width
    gains = norm_gains.astype(jnp.float32)
    shifts = norm_shifts.astype(jnp.float32)
    segment = segment_ids(seq_lens[0], count)
    resid = tokens.astype(jnp.float32)
    dy_full = cotangent.astype(jnp.float32)
    qkv_full, out_full = (
        lax.all_gather(w_qkv, "wide", axis=1, tiled=True),
        lax.all_gather(w_attn_out, "wide", axis=1, tiled=True),
    )
    normed_low = layer_norm(resid, gains[0], shifts[0]).astype(jnp.bfloat16)
    proj = jnp.einsum(
        "td,jde->jte", normed_low, qkv_full, preferred_element_type=jnp.float32
    ).astype(jnp.bfloat16)
    query, key, value = (proj[0], proj[1], proj[2])
    attended, logsum = attend_forward(query, key, value, segment)
    attended_low = attended.astype(jnp.bfloat16)
    mixed = jnp.dot(attended_low, out_full, preferred_element_type=jnp.float32)
    mixed_mine = lax.psum_scatter(mixed, "narrow", scatter_dimension=1, tiled=True)
    middle_mine = lax.dynamic_slice_in_dim(resid, first_col, width, 1) + mixed_mine
    middle = lax.all_gather(middle_mine, "narrow", axis=1, tiled=True)
    normed_two = layer_norm(middle, gains[1], shifts[1])
    ffn_in_part, ffn_down_part = (
        lax.all_gather(w_ffn_in, "wide", axis=1, tiled=True),
        lax.all_gather(w_ffn_down, "wide", axis=1, tiled=True),
    )
    dy_cols = lax.dynamic_slice_in_dim(cotangent, first_col, width, 1)
    normed_mine = lax.dynamic_slice_in_dim(normed_two, first_col, width, 1).astype(jnp.bfloat16)
    starts = jnp.arange(count // FBLK, dtype=jnp.int32) * FBLK

    def ffn_forward(carry, start):
        x_block, share, act_rows = hidden_block(normed_mine, ffn_in_part, start)
        result = lax.dot_general(
            act_rows, ffn_down_part, (((1,), (1,)), ((), ())), preferred_element_type=jnp.float32
        )
        return (carry, result)

    _, branch = lax.scan(ffn_forward, jnp.zeros((), jnp.float32), starts)
    branch_full = lax.all_gather(
        branch.reshape(count, width).astype(jnp.bfloat16), "narrow", axis=1, tiled=True
    ).astype(jnp.float32)
    layer_out = (middle + branch_full).astype(jnp.bfloat16)

    def ffn_backward(carry, start):
        grad_in, grad_down = carry
        x_block, share, act_rows = hidden_block(normed_mine, ffn_in_part, start)
        dy_block = lax.dynamic_slice_in_dim(dy_cols, start, FBLK, 0)
        dact = lax.psum_scatter(
            jnp.dot(dy_block, ffn_down_part, preferred_element_type=jnp.float32),
            "narrow",
            scatter_dimension=0,
            tiled=True,
        )
        _, gelu_back = jax.vjp(partial(jax.nn.gelu, approximate=False), share)
        dshare = gelu_back(dact)[0].astype(jnp.bfloat16)
        drows = lax.all_gather(dshare, "narrow", axis=0, tiled=True)
        grad_in = grad_in + lax.dot_general(
            x_block, drows, (((0,), (0,)), ((), ())), preferred_element_type=jnp.float32
        )
        grad_down = grad_down + lax.dot_general(
            dy_block, act_rows, (((0,), (0,)), ((), ())), preferred_element_type=jnp.float32
        )
        dnormed = lax.dot_general(
            drows, ffn_in_part, (((1,), (1,)), ((), ())), preferred_element_type=jnp.float32
        )
        return ((grad_in, grad_down), dnormed)

    empty = jnp.zeros(ffn_in_part.shape, jnp.float32)
    (grad_in, grad_down), dnormed = lax.scan(ffn_backward, (empty, empty), starts)
    dnormed_two = lax.all_gather(dnormed.reshape(count, width), "narrow", axis=1, tiled=True)
    grad_in_out, grad_down_out = (
        lax.psum_scatter(grad_in, "wide", scatter_dimension=1, tiled=True),
        lax.psum_scatter(grad_down, "wide", scatter_dimension=1, tiled=True),
    )
    _, norm_back_two = jax.vjp(layer_norm, middle, gains[1], shifts[1])
    dmiddle, dgain_two, dshift_two = norm_back_two(dnormed_two)
    dmiddle = dmiddle + dy_full
    dmixed_low = dmiddle.astype(jnp.bfloat16)
    grad_out = lax.dot_general(
        attended_low, dmixed_low, (((0,), (0,)), ((), ())), preferred_element_type=jnp.float32
    )
    dattended = lax.dot_general(
        dmixed_low, out_full, (((1,), (1,)), ((), ())), preferred_element_type=jnp.float32
    ).astype(jnp.bfloat16)
    dquery, dkey, dvalue = attend_backward(query, key, value, dattended, logsum, segment)
    dproj = jnp.stack([dquery, dkey, dvalue]).astype(jnp.bfloat16)
    grad_proj = jnp.einsum("td,jte->jde", normed_low, dproj, preferred_element_type=jnp.float32)
    dnormed_part = jnp.einsum("jte,jde->td", dproj, qkv_full, preferred_element_type=jnp.float32)
    dnormed_one = lax.psum(dnormed_part.astype(jnp.bfloat16), "narrow").astype(jnp.float32)
    _, norm_back_one = jax.vjp(layer_norm, resid, gains[0], shifts[0])
    dresid, dgain_one, dshift_one = norm_back_one(dnormed_one)
    input_grad = (dmiddle + dresid).astype(jnp.bfloat16)
    dgains = jnp.stack([dgain_one, dgain_two])
    dshifts = jnp.stack([dshift_one, dshift_two])
    gain_out, shift_out, proj_out, attn_out = (
        lax.psum_scatter(dgains, "wide", scatter_dimension=1, tiled=True),
        lax.psum_scatter(dshifts, "wide", scatter_dimension=1, tiled=True),
        lax.psum_scatter(grad_proj, "wide", scatter_dimension=1, tiled=True),
        lax.psum_scatter(grad_out, "wide", scatter_dimension=1, tiled=True),
    )
    return (
        layer_out,
        input_grad,
        gain_out,
        shift_out,
        proj_out,
        attn_out,
        grad_in_out,
        grad_down_out,
    )


def solution(mesh):
    placed = (
        P("wide", None),
        P("wide", None),
        P("wide", None),
        P(),
        P(),
        P(None, "wide", "narrow"),
        P("narrow", "wide"),
        P("narrow", "wide"),
        P("narrow", "wide"),
    )
    return jax.shard_map(
        local,
        mesh=mesh,
        in_specs=placed,
        out_specs=(
            P("wide", None),
            P("wide", None),
            P(None, "wide"),
            P(None, "wide"),
            P(None, "wide", "narrow"),
            P("narrow", "wide"),
            P("narrow", "wide"),
            P("narrow", "wide"),
        ),
        check_vma=False,
    )
```

profile of v0, /device:TPU:0, one launch (start us, length us, event | category | flops | bytes accessed | tf_op | source)
XLA Modules:
  0.0 4609.1 jit_solution(13928919483076880924)
XLA Ops:
  36.1 182.4 %while.84 = (s32[]{:T(128)}, bf16[5,1536,32]{1,2,0:T(8,128)(2,1)}, f32[5,1536]{1,0:T(8,128)}, s32[5]{0:T(128)}, bf16[1536,160]{1,0:T(8,128)(2,1)}, /*index=5*/bf...) while((s32[]{:T(128)}, bf16[5,1536,32]{1,2,0:T(8,128)(2,1)}, ...), condition=%wide.region_9.10_spmd.clone, body=%wide.region_4.9_spmd.clone.sunk | while | flops 107740680 | bytes 11363814 | solution.py:55
  236.6 69.2 %reduce-scatter.19.cloned.1.call-done = f32[1536,160]{0,1:T(8,128)} async-done(((f32[1536,640]{0,1:T(8,128)}), f32[1536,160]{0,1:T(8,128)}) %reduce-scatter.19.cloned.1.call-update) | async-done | bytes 983056 | tf_op jit(solution)/shard_map/reduce_scatter | solution.py:141
  312.1 73.2 %all-gather.9.cloned.1.call-done = f32[1536,640]{0,1:T(8,128)} async-done(((f32[1536,160]{0,1:T(8,128)}), f32[1536,640]{0,1:T(8,128)}) %all-gather.9.cloned.1.call-update) | async-done | bytes 3932176 | tf_op jit(solution)/shard_map/all_gather | solution.py:143
  439.6 2218.3 %while.87 = (s32[]{:T(128)}, f32[160,5120]{1,0:T(8,128)}, f32[160,5120]{1,0:T(8,128)}, f32[12,128,160]{1,0,2:T(8,128)}, s32[12]{0:T(128)S(1)}, /*index=5*/bf16[1...) while((s32[]{:T(128)}, f32[160,5120]{1,0:T(8,128)}, ...), condition=%wide.region_19.20_spmd.clone, body=%wide.region_16.19_spmd.clone.sunk | while | flops 1064796160 | bytes 83411448 | solution.py:191
  448.0 50.1 %reduce-scatter.37.cloned.1.call-done = f32[32,5120]{1,0:T(8,128)} async-done(((f32[128,5120]{1,0:T(8,128)}), f32[32,5120]{1,0:T(8,128)}) %reduce-scatter.37.cloned.1.call-update) | async-done | bytes 655376 | tf_op jit(solution)/shard_map/while/body/eval_jaxpr/reduce_scatter | solution.py:107
  501.3 50.8 %reduce-scatter.35.cloned.1.call-done = f32[32,5120]{1,0:T(8,128)} async-done(((f32[128,5120]{1,0:T(8,128)}), f32[32,5120]{1,0:T(8,128)}) %reduce-scatter.35.cloned.1.call-update) | async-done | bytes 655376 | tf_op jit(solution)/shard_map/while/body/eval_jaxpr/reduce_scatter | solution.py:170
  632.9 49.1 %reduce-scatter.37.cloned.1.call-done = f32[32,5120]{1,0:T(8,128)} async-done(((f32[128,5120]{1,0:T(8,128)}), f32[32,5120]{1,0:T(8,128)}) %reduce-scatter.37.cloned.1.call-update) | async-done | bytes 655376 | tf_op jit(solution)/shard_map/while/body/eval_jaxpr/reduce_scatter | solution.py:107
  685.1 50.8 %reduce-scatter.35.cloned.1.call-done = f32[32,5120]{1,0:T(8,128)} async-done(((f32[128,5120]{1,0:T(8,128)}), f32[32,5120]{1,0:T(8,128)}) %reduce-scatter.35.cloned.1.call-update) | async-done | bytes 655376 | tf_op jit(solution)/shard_map/while/body/eval_jaxpr/reduce_scatter | solution.py:170
  817.6 49.1 %reduce-scatter.37.cloned.1.call-done = f32[32,5120]{1,0:T(8,128)} async-done(((f32[128,5120]{1,0:T(8,128)}), f32[32,5120]{1,0:T(8,128)}) %reduce-scatter.37.cloned.1.call-update) | async-done | bytes 655376 | tf_op jit(solution)/shard_map/while/body/eval_jaxpr/reduce_scatter | solution.py:107
  869.9 50.8 %reduce-scatter.35.cloned.1.call-done = f32[32,5120]{1,0:T(8,128)} async-done(((f32[128,5120]{1,0:T(8,128)}), f32[32,5120]{1,0:T(8,128)}) %reduce-scatter.35.cloned.1.call-update) | async-done | bytes 655376 | tf_op jit(solution)/shard_map/while/body/eval_jaxpr/reduce_scatter | solution.py:170
  1002.3 49.1 %reduce-scatter.37.cloned.1.call-done = f32[32,5120]{1,0:T(8,128)} async-done(((f32[128,5120]{1,0:T(8,128)}), f32[32,5120]{1,0:T(8,128)}) %reduce-scatter.37.cloned.1.call-update) | async-done | bytes 655376 | tf_op jit(solution)/shard_map/while/body/eval_jaxpr/reduce_scatter | solution.py:107
  1054.6 50.8 %reduce-scatter.35.cloned.1.call-done = f32[32,5120]{1,0:T(8,128)} async-done(((f32[128,5120]{1,0:T(8,128)}), f32[32,5120]{1,0:T(8,128)}) %reduce-scatter.35.cloned.1.call-update) | async-done | bytes 655376 | tf_op jit(solution)/shard_map/while/body/eval_jaxpr/reduce_scatter | solution.py:170
  1187.0 49.1 %reduce-scatter.37.cloned.1.call-done = f32[32,5120]{1,0:T(8,128)} async-done(((f32[128,5120]{1,0:T(8,128)}), f32[32,5120]{1,0:T(8,128)}) %reduce-scatter.37.cloned.1.call-update) | async-done | bytes 655376 | tf_op jit(solution)/shard_map/while/body/eval_jaxpr/reduce_scatter | solution.py:107
  1239.3 50.9 %reduce-scatter.35.cloned.1.call-done = f32[32,5120]{1,0:T(8,128)} async-done(((f32[128,5120]{1,0:T(8,128)}), f32[32,5120]{1,0:T(8,128)}) %reduce-scatter.35.cloned.1.call-update) | async-done | bytes 655376 | tf_op jit(solution)/shard_map/while/body/eval_jaxpr/reduce_scatter | solution.py:170
  1371.9 49.1 %reduce-scatter.37.cloned.1.call-done = f32[32,5120]{1,0:T(8,128)} async-done(((f32[128,5120]{1,0:T(8,128)}), f32[32,5120]{1,0:T(8,128)}) %reduce-scatter.37.cloned.1.call-update) | async-done | bytes 655376 | tf_op jit(solution)/shard_map/while/body/eval_jaxpr/reduce_scatter | solution.py:107
  1424.2 50.8 %reduce-scatter.35.cloned.1.call-done = f32[32,5120]{1,0:T(8,128)} async-done(((f32[128,5120]{1,0:T(8,128)}), f32[32,5120]{1,0:T(8,128)}) %reduce-scatter.35.cloned.1.call-update) | async-done | bytes 655376 | tf_op jit(solution)/shard_map/while/body/eval_jaxpr/reduce_scatter | solution.py:170
  1556.8 49.1 %reduce-scatter.37.cloned.1.call-done = f32[32,5120]{1,0:T(8,128)} async-done(((f32[128,5120]{1,0:T(8,128)}), f32[32,5120]{1,0:T(8,128)}) %reduce-scatter.37.cloned.1.call-update) | async-done | bytes 655376 | tf_op jit(solution)/shard_map/while/body/eval_jaxpr/reduce_scatter | solution.py:107
  1609.1 50.8 %reduce-scatter.35.cloned.1.call-done = f32[32,5120]{1,0:T(8,128)} async-done(((f32[128,5120]{1,0:T(8,128)}), f32[32,5120]{1,0:T(8,128)}) %reduce-scatter.35.cloned.1.call-update) | async-done | bytes 655376 | tf_op jit(solution)/shard_map/while/body/eval_jaxpr/reduce_scatter | solution.py:170
  1741.7 49.1 %reduce-scatter.37.cloned.1.call-done = f32[32,5120]{1,0:T(8,128)} async-done(((f32[128,5120]{1,0:T(8,128)}), f32[32,5120]{1,0:T(8,128)}) %reduce-scatter.37.cloned.1.call-update) | async-done | bytes 655376 | tf_op jit(solution)/shard_map/while/body/eval_jaxpr/reduce_scatter | solution.py:107
  1794.0 50.9 %reduce-scatter.35.cloned.1.call-done = f32[32,5120]{1,0:T(8,128)} async-done(((f32[128,5120]{1,0:T(8,128)}), f32[32,5120]{1,0:T(8,128)}) %reduce-scatter.35.cloned.1.call-update) | async-done | bytes 655376 | tf_op jit(solution)/shard_map/while/body/eval_jaxpr/reduce_scatter | solution.py:170
  1926.5 49.1 %reduce-scatter.37.cloned.1.call-done = f32[32,5120]{1,0:T(8,128)} async-done(((f32[128,5120]{1,0:T(8,128)}), f32[32,5120]{1,0:T(8,128)}) %reduce-scatter.37.cloned.1.call-update) | async-done | bytes 655376 | tf_op jit(solution)/shard_map/while/body/eval_jaxpr/reduce_scatter | solution.py:107
  1978.8 50.9 %reduce-scatter.35.cloned.1.call-done = f32[32,5120]{1,0:T(8,128)} async-done(((f32[128,5120]{1,0:T(8,128)}), f32[32,5120]{1,0:T(8,128)}) %reduce-scatter.35.cloned.1.call-update) | async-done | bytes 655376 | tf_op jit(solution)/shard_map/while/body/eval_jaxpr/reduce_scatter | solution.py:170
  2111.5 49.1 %reduce-scatter.37.cloned.1.call-done = f32[32,5120]{1,0:T(8,128)} async-done(((f32[128,5120]{1,0:T(8,128)}), f32[32,5120]{1,0:T(8,128)}) %reduce-scatter.37.cloned.1.call-update) | async-done | bytes 655376 | tf_op jit(solution)/shard_map/while/body/eval_jaxpr/reduce_scatter | solution.py:107
  2163.8 50.9 %reduce-scatter.35.cloned.1.call-done = f32[32,5120]{1,0:T(8,128)} async-done(((f32[128,5120]{1,0:T(8,128)}), f32[32,5120]{1,0:T(8,128)}) %reduce-scatter.35.cloned.1.call-update) | async-done | bytes 655376 | tf_op jit(solution)/shard_map/while/body/eval_jaxpr/reduce_scatter | solution.py:170
  2296.6 49.1 %reduce-scatter.37.cloned.1.call-done = f32[32,5120]{1,0:T(8,128)} async-done(((f32[128,5120]{1,0:T(8,128)}), f32[32,5120]{1,0:T(8,128)}) %reduce-scatter.37.cloned.1.call-update) | async-done | bytes 655376 | tf_op jit(solution)/shard_map/while/body/eval_jaxpr/reduce_scatter | solution.py:107
  2348.9 50.8 %reduce-scatter.35.cloned.1.call-done = f32[32,5120]{1,0:T(8,128)} async-done(((f32[128,5120]{1,0:T(8,128)}), f32[32,5120]{1,0:T(8,128)}) %reduce-scatter.35.cloned.1.call-update) | async-done | bytes 655376 | tf_op jit(solution)/shard_map/while/body/eval_jaxpr/reduce_scatter | solution.py:170
  2481.3 49.1 %reduce-scatter.37.cloned.1.call-done = f32[32,5120]{1,0:T(8,128)} async-done(((f32[128,5120]{1,0:T(8,128)}), f32[32,5120]{1,0:T(8,128)}) %reduce-scatter.37.cloned.1.call-update) | async-done | bytes 655376 | tf_op jit(solution)/shard_map/while/body/eval_jaxpr/reduce_scatter | solution.py:107
  2533.6 50.9 %reduce-scatter.35.cloned.1.call-done = f32[32,5120]{1,0:T(8,128)} async-done(((f32[128,5120]{1,0:T(8,128)}), f32[32,5120]{1,0:T(8,128)}) %reduce-scatter.35.cloned.1.call-update) | async-done | bytes 655376 | tf_op jit(solution)/shard_map/while/body/eval_jaxpr/reduce_scatter | solution.py:170
  2660.5 1148.4 %while.82 = (s32[]{:T(128)}, bf16[12,128,160]{1,2,0:T(8,128)(2,1)}, s32[12]{0:T(128)S(1)}, bf16[1536,160]{1,0:T(8,128)(2,1)}, bf16[160,5120]{1,0:T(8,128)(2,1)},...) while((s32[]{:T(128)}, bf16[12,128,160]{1,2,0:T(8,128)(2,1)}, s32[12]{0:T(128)S(1)}, ...), condition=%wide.region_15.16_spmd, body=%wide.region_13.15_spmd.sunk | while | flops 430080000 | bytes 29638920 | solution.py:160
  2666.7 51.2 %reduce-scatter.33.cloned.1.call-done = f32[32,5120]{1,0:T(8,128)} async-done(((f32[128,5120]{1,0:T(8,128)}), f32[32,5120]{1,0:T(8,128)}) %reduce-scatter.33.cloned.1.call-update) | async-done | bytes 655376 | tf_op jit(solution)/shard_map/while/body/eval_jaxpr/reduce_scatter | solution.py:107
  2762.4 51.2 %reduce-scatter.33.cloned.1.call-done = f32[32,5120]{1,0:T(8,128)} async-done(((f32[128,5120]{1,0:T(8,128)}), f32[32,5120]{1,0:T(8,128)}) %reduce-scatter.33.cloned.1.call-update) | async-done | bytes 655376 | tf_op jit(solution)/shard_map/while/body/eval_jaxpr/reduce_scatter | solution.py:107
  2858.2 51.2 %reduce-scatter.33.cloned.1.call-done = f32[32,5120]{1,0:T(8,128)} async-done(((f32[128,5120]{1,0:T(8,128)}), f32[32,5120]{1,0:T(8,128)}) %reduce-scatter.33.cloned.1.call-update) | async-done | bytes 655376 | tf_op jit(solution)/shard_map/while/body/eval_jaxpr/reduce_scatter | solution.py:107
  2953.9 51.2 %reduce-scatter.33.cloned.1.call-done = f32[32,5120]{1,0:T(8,128)} async-done(((f32[128,5120]{1,0:T(8,128)}), f32[32,5120]{1,0:T(8,128)}) %reduce-scatter.33.cloned.1.call-update) | async-done | bytes 655376 | tf_op jit(solution)/shard_map/while/body/eval_jaxpr/reduce_scatter | solution.py:107
  3049.6 51.2 %reduce-scatter.33.cloned.1.call-done = f32[32,5120]{1,0:T(8,128)} async-done(((f32[128,5120]{1,0:T(8,128)}), f32[32,5120]{1,0:T(8,128)}) %reduce-scatter.33.cloned.1.call-update) | async-done | bytes 655376 | tf_op jit(solution)/shard_map/while/body/eval_jaxpr/reduce_scatter | solution.py:107
  3145.3 51.2 %reduce-scatter.33.cloned.1.call-done = f32[32,5120]{1,0:T(8,128)} async-done(((f32[128,5120]{1,0:T(8,128)}), f32[32,5120]{1,0:T(8,128)}) %reduce-scatter.33.cloned.1.call-update) | async-done | bytes 655376 | tf_op jit(solution)/shard_map/while/body/eval_jaxpr/reduce_scatter | solution.py:107
  3241.0 51.2 %reduce-scatter.33.cloned.1.call-done = f32[32,5120]{1,0:T(8,128)} async-done(((f32[128,5120]{1,0:T(8,128)}), f32[32,5120]{1,0:T(8,128)}) %reduce-scatter.33.cloned.1.call-update) | async-done | bytes 655376 | tf_op jit(solution)/shard_map/while/body/eval_jaxpr/reduce_scatter | solution.py:107
  3336.7 51.2 %reduce-scatter.33.cloned.1.call-done = f32[32,5120]{1,0:T(8,128)} async-done(((f32[128,5120]{1,0:T(8,128)}), f32[32,5120]{1,0:T(8,128)}) %reduce-scatter.33.cloned.1.call-update) | async-done | bytes 655376 | tf_op jit(solution)/shard_map/while/body/eval_jaxpr/reduce_scatter | solution.py:107
  3432.4 51.2 %reduce-scatter.33.cloned.1.call-done = f32[32,5120]{1,0:T(8,128)} async-done(((f32[128,5120]{1,0:T(8,128)}), f32[32,5120]{1,0:T(8,128)}) %reduce-scatter.33.cloned.1.call-update) | async-done | bytes 655376 | tf_op jit(solution)/shard_map/while/body/eval_jaxpr/reduce_scatter | solution.py:107
  3528.1 51.2 %reduce-scatter.33.cloned.1.call-done = f32[32,5120]{1,0:T(8,128)} async-done(((f32[128,5120]{1,0:T(8,128)}), f32[32,5120]{1,0:T(8,128)}) %reduce-scatter.33.cloned.1.call-update) | async-done | bytes 655376 | tf_op jit(solution)/shard_map/while/body/eval_jaxpr/reduce_scatter | solution.py:107
  3623.8 51.2 %reduce-scatter.33.cloned.1.call-done = f32[32,5120]{1,0:T(8,128)} async-done(((f32[128,5120]{1,0:T(8,128)}), f32[32,5120]{1,0:T(8,128)}) %reduce-scatter.33.cloned.1.call-update) | async-done | bytes 655376 | tf_op jit(solution)/shard_map/while/body/eval_jaxpr/reduce_scatter | solution.py:107
  3719.5 51.2 %reduce-scatter.33.cloned.1.call-done = f32[32,5120]{1,0:T(8,128)} async-done(((f32[128,5120]{1,0:T(8,128)}), f32[32,5120]{1,0:T(8,128)}) %reduce-scatter.33.cloned.1.call-update) | async-done | bytes 655376 | tf_op jit(solution)/shard_map/while/body/eval_jaxpr/reduce_scatter | solution.py:107
  3814.6 72.3 %all-gather.17.cloned.1.call-done = f32[1536,640]{0,1:T(8,128)} async-done(((f32[1536,160]{0,1:T(8,128)}), f32[1536,640]{0,1:T(8,128)}) %all-gather.17.cloned.1.call-update) | async-done | bytes 3932176 | tf_op jit(solution)/shard_map/all_gather | solution.py:192
  3942.7 319.0 %while.86 = (s32[]{:T(128)}, bf16[5,1536,32]{2,1,0:T(8,128)(2,1)}, bf16[5,1536,32]{1,2,0:T(8,128)(2,1)}, bf16[5,1536,32]{1,2,0:T(8,128)(2,1)}, s32[5]{0:T(128)},...) while((s32[]{:T(128)}, bf16[5,1536,32]{2,1,0:T(8,128)(2,1)}, ...), condition=%wide.region_26.27_spmd.clone, body=%wide.region_22.26_spmd.clone.sunk | while | flops 259784208 | bytes 27660404 | solution.py:97
  4018.4 48.4 %while.89 = (s32[]{:T(128)}, f32[1536,32]{0,1:T(8,128)}, f32[1536,32]{0,1:T(8,128)}, bf16[3,512,32]{1,2,0:T(8,128)(2,1)}, s32[3]{0:T(128)}, /*index=5*/s32[1536]...) while((s32[]{:T(128)}, f32[1536,32]{0,1:T(8,128)}, ...), condition=%wide.region_25.25_spmd.clone, body=%wide.region_23.24_spmd.clone.sunk | while | flops 259784192 | bytes 25385684 | solution.py:94
  4146.0 48.4 %while.89 = (s32[]{:T(128)}, f32[1536,32]{0,1:T(8,128)}, f32[1536,32]{0,1:T(8,128)}, bf16[3,512,32]{1,2,0:T(8,128)(2,1)}, s32[3]{0:T(128)}, /*index=5*/s32[1536]...) while((s32[]{:T(128)}, f32[1536,32]{0,1:T(8,128)}, ...), condition=%wide.region_25.25_spmd.clone, body=%wide.region_23.24_spmd.clone.sunk | while | flops 259784192 | bytes 25385684 | solution.py:94
  4281.8 67.5 %all-reduce.2.cloned.1.call-done = bf16[1536,640]{0,1:T(8,128)(2,1)} async-done(((bf16[1536,640]{0,1:T(8,128)(2,1)}), bf16[1536,640]{0,1:T(8,128)(2,1)}) %all-reduce.2.cloned.1.call-update) | async-done | bytes 1966096 | tf_op jit(solution)/shard_map/psum | solution.py:211
  4502.1 49.3 %reduce-scatter.21.cloned.1.call-done = f32[160,640]{1,0:T(8,128)} async-done(((f32[160,5120]{1,0:T(8,128)}), f32[160,640]{1,0:T(8,128)}) %reduce-scatter.21.cloned.1.call-update) | async-done | bytes 409616 | tf_op jit(solution)/shard_map/reduce_scatter | solution.py:194
  4551.5 50.9 %reduce-scatter.23.cloned.1.call-done = f32[160,640]{1,0:T(8,128)} async-done(((f32[160,5120]{1,0:T(8,128)}), f32[160,640]{1,0:T(8,128)}) %reduce-scatter.23.cloned.1.call-update) | async-done | bytes 409616 | tf_op jit(solution)/shard_map/reduce_scatter | solution.py:195
  (1024 shorter events, 2553.3 us)
Async XLA Ops:
  7.2 298.6 %reduce-scatter.19.cloned.1.call-start = ((), (), s32[]{:S(2)}) async-start(), calls=%async_computation.10 | async-start | bytes 4915200 | tf_op jit(solution)/shard_map/reduce_scatter | solution.py:141
  232.6 152.7 %all-gather.9.cloned.1.call-start = ((), (), s32[]{:S(2)}) async-start(), calls=%async_computation.11 | async-start | bytes 4915200 | tf_op jit(solution)/shard_map/all_gather | solution.py:143
  308.3 103.5 %all-gather.11.cloned.1.call-start = ((), (), s32[]{:S(2)}) async-start(), calls=%async_computation.12 | async-start | bytes 1843200 | tf_op jit(solution)/shard_map/all_gather | solution.py:146
  309.1 130.5 %all-gather.13.cloned.1.call-start = ((), (), s32[]{:S(2)}) async-start(), calls=%async_computation.13 | async-start | bytes 1843200 | tf_op jit(solution)/shard_map/all_gather | solution.py:147
  445.8 106.3 %reduce-scatter.35.cloned.1.call-start = ((), (), s32[]{:S(2)}) async-start(), calls=%async_computation.25 | async-start | bytes 3276800 | tf_op jit(solution)/shard_map/while/body/eval_jaxpr/reduce_scatter | solution.py:170
  447.9 139.0 %all-gather.21.cloned.1.call-start = ((), (), s32[]{:S(2)}) async-start(), calls=%async_computation.27 | async-start | bytes 1638400 | tf_op jit(solution)/shard_map/while/body/eval_jaxpr/all_gather | solution.py:178
  630.7 105.2 %reduce-scatter.35.cloned.1.call-start = ((), (), s32[]{:S(2)}) async-start(), calls=%async_computation.25 | async-start | bytes 3276800 | tf_op jit(solution)/shard_map/while/body/eval_jaxpr/reduce_scatter | solution.py:170
  632.8 138.0 %all-gather.21.cloned.1.call-start = ((), (), s32[]{:S(2)}) async-start(), calls=%async_computation.27 | async-start | bytes 1638400 | tf_op jit(solution)/shard_map/while/body/eval_jaxpr/all_gather | solution.py:178
  815.4 105.2 %reduce-scatter.35.cloned.1.call-start = ((), (), s32[]{:S(2)}) async-start(), calls=%async_computation.25 | async-start | bytes 3276800 | tf_op jit(solution)/shard_map/while/body/eval_jaxpr/reduce_scatter | solution.py:170
  817.5 138.0 %all-gather.21.cloned.1.call-start = ((), (), s32[]{:S(2)}) async-start(), calls=%async_computation.27 | async-start | bytes 1638400 | tf_op jit(solution)/shard_map/while/body/eval_jaxpr/all_gather | solution.py:178
  1000.1 105.2 %reduce-scatter.35.cloned.1.call-start = ((), (), s32[]{:S(2)}) async-start(), calls=%async_computation.25 | async-start | bytes 3276800 | tf_op jit(solution)/shard_map/while/body/eval_jaxpr/reduce_scatter | solution.py:170
  1002.3 138.0 %all-gather.21.cloned.1.call-start = ((), (), s32[]{:S(2)}) async-start(), calls=%async_computation.27 | async-start | bytes 1638400 | tf_op jit(solution)/shard_map/while/body/eval_jaxpr/all_gather | solution.py:178
  1184.9 105.4 %reduce-scatter.35.cloned.1.call-start = ((), (), s32[]{:S(2)}) async-start(), calls=%async_computation.25 | async-start | bytes 3276800 | tf_op jit(solution)/shard_map/while/body/eval_jaxpr/reduce_scatter | solution.py:170
  1187.0 138.1 %all-gather.21.cloned.1.call-start = ((), (), s32[]{:S(2)}) async-start(), calls=%async_computation.27 | async-start | bytes 1638400 | tf_op jit(solution)/shard_map/while/body/eval_jaxpr/all_gather | solution.py:178
  1369.7 105.2 %reduce-scatter.35.cloned.1.call-start = ((), (), s32[]{:S(2)}) async-start(), calls=%async_computation.25 | async-start | bytes 3276800 | tf_op jit(solution)/shard_map/while/body/eval_jaxpr/reduce_scatter | solution.py:170
  1371.9 138.0 %all-gather.21.cloned.1.call-start = ((), (), s32[]{:S(2)}) async-start(), calls=%async_computation.27 | async-start | bytes 1638400 | tf_op jit(solution)/shard_map/while/body/eval_jaxpr/all_gather | solution.py:178
  1554.6 105.2 %reduce-scatter.35.cloned.1.call-start = ((), (), s32[]{:S(2)}) async-start(), calls=%async_computation.25 | async-start | bytes 3276800 | tf_op jit(solution)/shard_map/while/body/eval_jaxpr/reduce_scatter | solution.py:170
  1556.7 138.0 %all-gather.21.cloned.1.call-start = ((), (), s32[]{:S(2)}) async-start(), calls=%async_computation.27 | async-start | bytes 1638400 | tf_op jit(solution)/shard_map/while/body/eval_jaxpr/all_gather | solution.py:178
  1739.5 105.4 %reduce-scatter.35.cloned.1.call-start = ((), (), s32[]{:S(2)}) async-start(), calls=%async_computation.25 | async-start | bytes 3276800 | tf_op jit(solution)/shard_map/while/body/eval_jaxpr/reduce_scatter | solution.py:170
  1741.6 138.1 %all-gather.21.cloned.1.call-start = ((), (), s32[]{:S(2)}) async-start(), calls=%async_computation.27 | async-start | bytes 1638400 | tf_op jit(solution)/shard_map/while/body/eval_jaxpr/all_gather | solution.py:178
  1924.3 105.4 %reduce-scatter.35.cloned.1.call-start = ((), (), s32[]{:S(2)}) async-start(), calls=%async_computation.25 | async-start | bytes 3276800 | tf_op jit(solution)/shard_map/while/body/eval_jaxpr/reduce_scatter | solution.py:170
  1926.5 138.1 %all-gather.21.cloned.1.call-start = ((), (), s32[]{:S(2)}) async-start(), calls=%async_computation.27 | async-start | bytes 1638400 | tf_op jit(solution)/shard_map/while/body/eval_jaxpr/all_gather | solution.py:178
  2109.4 105.4 %reduce-scatter.35.cloned.1.call-start = ((), (), s32[]{:S(2)}) async-start(), calls=%async_computation.25 | async-start | bytes 3276800 | tf_op jit(solution)/shard_map/while/body/eval_jaxpr/reduce_scatter | solution.py:170
  2111.5 138.1 %all-gather.21.cloned.1.call-start = ((), (), s32[]{:S(2)}) async-start(), calls=%async_computation.27 | async-start | bytes 1638400 | tf_op jit(solution)/shard_map/while/body/eval_jaxpr/all_gather | solution.py:178
  2294.4 105.3 %reduce-scatter.35.cloned.1.call-start = ((), (), s32[]{:S(2)}) async-start(), calls=%async_computation.25 | async-start | bytes 3276800 | tf_op jit(solution)/shard_map/while/body/eval_jaxpr/reduce_scatter | solution.py:170
  2296.5 138.0 %all-gather.21.cloned.1.call-start = ((), (), s32[]{:S(2)}) async-start(), calls=%async_computation.27 | async-start | bytes 1638400 | tf_op jit(solution)/shard_map/while/body/eval_jaxpr/all_gather | solution.py:178
  2479.1 105.4 %reduce-scatter.35.cloned.1.call-start = ((), (), s32[]{:S(2)}) async-start(), calls=%async_computation.25 | async-start | bytes 3276800 | tf_op jit(solution)/shard_map/while/body/eval_jaxpr/reduce_scatter | solution.py:170
  2481.2 138.1 %all-gather.21.cloned.1.call-start = ((), (), s32[]{:S(2)}) async-start(), calls=%async_computation.27 | async-start | bytes 1638400 | tf_op jit(solution)/shard_map/while/body/eval_jaxpr/all_gather | solution.py:178
  2666.7 87.0 %all-gather.19.cloned.1.call-start = ((), (), s32[]{:S(2)}) async-start(), calls=%async_computation.24 | async-start | bytes 1638400 | tf_op jit(solution)/shard_map/while/body/eval_jaxpr/all_gather | solution.py:114
  2762.4 87.0 %all-gather.19.cloned.1.call-start = ((), (), s32[]{:S(2)}) async-start(), calls=%async_computation.24 | async-start | bytes 1638400 | tf_op jit(solution)/shard_map/while/body/eval_jaxpr/all_gather | solution.py:114
  2858.1 87.0 %all-gather.19.cloned.1.call-start = ((), (), s32[]{:S(2)}) async-start(), calls=%async_computation.24 | async-start | bytes 1638400 | tf_op jit(solution)/shard_map/while/body/eval_jaxpr/all_gather | solution.py:114
  2953.8 87.0 %all-gather.19.cloned.1.call-start = ((), (), s32[]{:S(2)}) async-start(), calls=%async_computation.24 | async-start | bytes 1638400 | tf_op jit(solution)/shard_map/while/body/eval_jaxpr/all_gather | solution.py:114
  3049.5 87.0 %all-gather.19.cloned.1.call-start = ((), (), s32[]{:S(2)}) async-start(), calls=%async_computation.24 | async-start | bytes 1638400 | tf_op jit(solution)/shard_map/while/body/eval_jaxpr/all_gather | solution.py:114
  3145.2 87.0 %all-gather.19.cloned.1.call-start = ((), (), s32[]{:S(2)}) async-start(), calls=%async_computation.24 | async-start | bytes 1638400 | tf_op jit(solution)/shard_map/while/body/eval_jaxpr/all_gather | solution.py:114
  3240.9 87.0 %all-gather.19.cloned.1.call-start = ((), (), s32[]{:S(2)}) async-start(), calls=%async_computation.24 | async-start | bytes 1638400 | tf_op jit(solution)/shard_map/while/body/eval_jaxpr/all_gather | solution.py:114
  3336.6 87.0 %all-gather.19.cloned.1.call-start = ((), (), s32[]{:S(2)}) async-start(), calls=%async_computation.24 | async-start | bytes 1638400 | tf_op jit(solution)/shard_map/while/body/eval_jaxpr/all_gather | solution.py:114
  3432.3 87.0 %all-gather.19.cloned.1.call-start = ((), (), s32[]{:S(2)}) async-start(), calls=%async_computation.24 | async-start | bytes 1638400 | tf_op jit(solution)/shard_map/while/body/eval_jaxpr/all_gather | solution.py:114
  3528.0 87.0 %all-gather.19.cloned.1.call-start = ((), (), s32[]{:S(2)}) async-start(), calls=%async_computation.24 | async-start | bytes 1638400 | tf_op jit(solution)/shard_map/while/body/eval_jaxpr/all_gather | solution.py:114
  3623.7 87.0 %all-gather.19.cloned.1.call-start = ((), (), s32[]{:S(2)}) async-start(), calls=%async_computation.24 | async-start | bytes 1638400 | tf_op jit(solution)/shard_map/while/body/eval_jaxpr/all_gather | solution.py:114
  3719.4 87.0 %all-gather.19.cloned.1.call-start = ((), (), s32[]{:S(2)}) async-start(), calls=%async_computation.24 | async-start | bytes 1638400 | tf_op jit(solution)/shard_map/while/body/eval_jaxpr/all_gather | solution.py:114
  3809.7 120.9 %all-gather.15.cloned.1.call-start = ((), (), s32[]{:S(2)}) async-start(), calls=%async_computation.14 | async-start | bytes 2457600 | tf_op jit(solution)/shard_map/all_gather | solution.py:161
  3811.6 537.6 %all-reduce.2.cloned.1.call-start = ((), (), s32[]{:S(2)}) async-start(), calls=%async_computation.16 | async-start | bytes 3932160 | tf_op jit(solution)/shard_map/psum | solution.py:211
  4268.3 117.7 %reduce-scatter.31.cloned.1.call-start = ((), (), s32[]{:S(2)}) async-start(), calls=%async_computation.22 | async-start | bytes 737280
  4271.6 155.6 %reduce-scatter.29.cloned.1.call-start = ((), (), s32[]{:S(2)}) async-start(), calls=%async_computation.21 | async-start | bytes 1474560
  4281.7 182.2 %reduce-scatter.27.cloned.1.call-start = ((), (), s32[]{:S(2)}) async-start(), calls=%async_computation.20 | async-start | bytes 368640
  4356.3 144.4 %reduce-scatter.25.cloned.1.call-start = ((), (), s32[]{:S(2)}) async-start(), calls=%async_computation.19 | async-start | bytes 368640
  4357.3 194.1 %reduce-scatter.21.cloned.1.call-start = ((), (), s32[]{:S(2)}) async-start(), calls=%async_computation.17 | async-start | bytes 3686400 | tf_op jit(solution)/shard_map/reduce_scatter | solution.py:194
  4357.9 244.4 %reduce-scatter.23.cloned.1.call-start = ((), (), s32[]{:S(2)}) async-start(), calls=%async_computation.18 | async-start | bytes 3686400 | tf_op jit(solution)/shard_map/reduce_scatter | solution.py:195
  (139 other events, 5984.7 us)
Sparse Core Ops, SparseCore 0:
  232.7 72.9 reduce-scatter.18
  308.5 76.8 all-gather.8
  445.9 52.0 reduce-scatter.36
  500.2 51.7 reduce-scatter.34
  630.8 51.0 reduce-scatter.36
  684.1 51.7 reduce-scatter.34
  815.5 51.0 reduce-scatter.36
  868.8 51.7 reduce-scatter.34
  1000.3 51.0 reduce-scatter.36
  1053.6 51.7 reduce-scatter.34
  1185.0 51.0 reduce-scatter.36
  1238.4 51.7 reduce-scatter.34
  1369.9 51.0 reduce-scatter.36
  1423.2 51.7 reduce-scatter.34
  1554.7 51.0 reduce-scatter.36
  1608.0 51.7 reduce-scatter.34
  1739.6 51.0 reduce-scatter.36
  1793.1 51.7 reduce-scatter.34
  1924.5 51.0 reduce-scatter.36
  1977.9 51.7 reduce-scatter.34
  2109.5 51.0 reduce-scatter.36
  2162.9 51.7 reduce-scatter.34
  2294.5 51.1 reduce-scatter.36
  2347.8 51.7 reduce-scatter.34
  2479.2 51.0 reduce-scatter.36
  2532.7 51.7 reduce-scatter.34
  2666.8 51.1 reduce-scatter.32
  2762.5 51.0 reduce-scatter.32
  2817.0 32.3 all-gather.18
  2858.2 51.0 reduce-scatter.32
  2953.9 51.0 reduce-scatter.32
  3049.6 51.0 reduce-scatter.32
  3145.3 51.0 reduce-scatter.32
  3241.0 51.0 reduce-scatter.32
  3336.7 51.0 reduce-scatter.32
  3432.4 51.0 reduce-scatter.32
  3528.1 51.0 reduce-scatter.32
  3623.9 51.0 reduce-scatter.32
  3719.6 51.0 reduce-scatter.32
  3811.4 75.4 all-gather.16
  3888.4 42.1 all-gather.14
  4268.5 80.7 all-reduce.1
  4352.4 33.5 reduce-scatter.30
  4389.8 37.3 reduce-scatter.28
  4430.1 33.7 reduce-scatter.26
  4466.9 33.7 reduce-scatter.24
  4504.6 46.8 reduce-scatter.20
  4555.4 46.8 reduce-scatter.22
  (37 shorter events, 1173.4 us)
where the time goes:
time: 4630 us; the launch traced here: 4610 us
  waiting for transfers between devices  3470 us (75%)
  matrix products  501 us (11%)
  local copies, waits for them, and re-layouts  284 us (6%)
  other arithmetic  192 us (4%)
  loops' own time  119 us (3%)
    reduce_scatter x24, waiting for transfers between devices, hidden_block(): lax.psum_scatter(jnp.dot(x_block, ffn_in_full, preferred_element_type=jnp...  1200 us
    all_gather x24, waiting for transfers between devices, hidden_block(): act_rows = lax.all_gather(act_share, 'narrow', axis=0, tiled=True)  675 us
    reduce_scatter x12, waiting for transfers between devices, ffn_backward(): lax.psum_scatter(jnp.dot(dy_block, ffn_down_part, preferred_element_type=...  610 us
    all_gather x12, waiting for transfers between devices, ffn_backward(): drows = lax.all_gather(dshare, 'narrow', axis=0, tiled=True)  382 us
    unnamed x17, waiting for transfers between devices  126 us
  transfers between devices with their start and end apart: 85, of which 85 were waited for; matrix products, arithmetic and copies ran while one was open for 5% of the time, Pallas kernels for 0%

commit v1 on v0

--- a/solution.py
+++ b/solution.py
@@ -8,6 +8,23 @@
 QBLK = 512
 FBLK = 128
 EPS = 1e-05
+
+
+def joined_along(parts, dim):
+    parts = jnp.moveaxis(parts, 0, dim)
+    dims = parts.shape
+    return parts.reshape(*dims[:dim], dims[dim] * dims[dim + 1], *dims[dim + 2 :])
+
+
+def doubled(shard, axis):
+    devices, here = (lax.axis_size(axis), lax.axis_index(axis))
+    blocks, stride = (shard[None], 1)
+    while stride < devices:
+        other = lax.ppermute(blocks, axis, [(i, i ^ stride) for i in range(devices)])
+        low = here & stride == 0
+        blocks = jnp.concatenate([jnp.where(low, blocks, other), jnp.where(low, other, blocks)])
+        stride *= 2
+    return blocks
 
 
 def layer_norm(rows, gain, shift):
@@ -111,7 +128,7 @@
         tiled=True,
     )
     act_share = jax.nn.gelu(share, approximate=False).astype(jnp.bfloat16)
-    act_rows = lax.all_gather(act_share, "narrow", axis=0, tiled=True)
+    act_rows = joined_along(doubled(act_share, "narrow"), 0)
     return (x_block, share, act_rows)
 
 

time: 4630 us -> 4730 us (1.022)
    all_gather x24 -> x0, waiting for transfers between devices: 675 us -> none  [hidden_block(): act_rows = lax.all_gather(act_share, 'narrow', axis=0, tiled=True)]
    ppermute x0 -> x48, waiting for transfers between devices: none -> 613 us  [doubled(): lax.ppermute(blocks, axis, [(i, i ^ stride) for i in range(devices)])]
    reduce_scatter x12, waiting for transfers between devices: 610 us -> 705 us  [ffn_backward(): lax.psum_scatter(jnp.dot(dy_block, ffn_down_part, preferred_element_type=...]
    convert_element_type x24 -> x0, other arithmetic: 76.8 us -> none  [hidden_block(): act_share = jax.nn.gelu(share, approximate=False).astype(jnp.bfloat16)]
    broadcast_in_dim x0 -> x24, other arithmetic: none -> 60.3 us  [doubled(): blocks, stride = (shard[None], 1)]
  transfers between devices with their start and end apart: 85 -> 109, of which waited for: 85 -> 99; matrix products, arithmetic and copies ran while one was open for 5% -> 4% of each run, Pallas kernels for 0% -> 0%
where the time goes in v1:
time: 4730 us; the launch traced here: 4710 us
  waiting for transfers between devices  3510 us (74%)
  matrix products  481 us (10%)
  local copies, waits for them, and re-layouts  283 us (6%)
  other arithmetic  223 us (5%)
  loops' own time  122 us (3%)
  starting transfers between devices  48.1 us (1%)
    reduce_scatter x24, waiting for transfers between devices, hidden_block(): lax.psum_scatter(jnp.dot(x_block, ffn_in_full, preferred_element_type=jnp...  1220 us
    reduce_scatter x12, waiting for transfers between devices, ffn_backward(): lax.psum_scatter(jnp.dot(dy_block, ffn_down_part, preferred_element_type=...  705 us
    ppermute x48, waiting for transfers between devices, doubled(): lax.ppermute(blocks, axis, [(i, i ^ stride) for i in range(devices)])  613 us
    all_gather x12, waiting for transfers between devices, ffn_backward(): drows = lax.all_gather(dshare, 'narrow', axis=0, tiled=True)  385 us
    unnamed x17, waiting for transfers between devices  126 us
  transfers between devices with their start and end apart: 109, of which 99 were waited for; matrix products, arithmetic and copies ran while one was open for 4% of the time, Pallas kernels for 0%

profile of v1, /device:TPU:0, one launch (start us, length us, event | category | flops | bytes accessed | tf_op | source)
XLA Modules:
  0.0 4710.4 jit_solution(15729508198978797958)
XLA Ops:
  36.1 184.5 %while.84 = (s32[]{:T(128)}, bf16[5,1536,32]{1,2,0:T(8,128)(2,1)}, f32[5,1536]{1,0:T(8,128)}, s32[5]{0:T(128)}, bf16[1536,160]{1,0:T(8,128)(2,1)}, /*index=5*/bf...) while((s32[]{:T(128)}, bf16[5,1536,32]{1,2,0:T(8,128)(2,1)}, ...), condition=%wide.region_9.10_spmd.clone, body=%wide.region_4.9_spmd.clone.sunk | while | flops 107740680 | bytes 11363814 | solution.py:72
  238.6 69.2 %reduce-scatter.19.cloned.1.call-done = f32[1536,160]{0,1:T(8,128)} async-done(((f32[1536,640]{0,1:T(8,128)}), f32[1536,160]{0,1:T(8,128)}) %reduce-scatter.19.cloned.1.call-update) | async-done | bytes 983056 | tf_op jit(solution)/shard_map/reduce_scatter | solution.py:158
  314.2 73.2 %all-gather.7.cloned.1.call-done = f32[1536,640]{0,1:T(8,128)} async-done(((f32[1536,160]{0,1:T(8,128)}), f32[1536,640]{0,1:T(8,128)}) %all-gather.7.cloned.1.call-update) | async-done | bytes 3932176 | tf_op jit(solution)/shard_map/all_gather | solution.py:160
  441.6 2196.1 %while.87 = (s32[]{:T(128)}, f32[160,5120]{1,0:T(8,128)}, f32[160,5120]{1,0:T(8,128)}, f32[12,128,160]{1,0,2:T(8,128)}, s32[12]{0:T(128)S(1)}, /*index=5*/bf16[1...) while((s32[]{:T(128)}, f32[160,5120]{1,0:T(8,128)}, ...), condition=%wide.region_19.20_spmd.clone, body=%wide.region_16.19_spmd.clone.sunk | while | flops 1067089920 | bytes 92914320 | solution.py:208
  450.6 50.1 %reduce-scatter.37.cloned.1.call-done = f32[32,5120]{1,0:T(8,128)} async-done(((f32[128,5120]{1,0:T(8,128)}), f32[32,5120]{1,0:T(8,128)}) %reduce-scatter.37.cloned.1.call-update) | async-done | bytes 655376 | tf_op jit(solution)/shard_map/while/body/eval_jaxpr/reduce_scatter | solution.py:124
  518.5 58.7 %reduce-scatter.35.cloned.1.call-done = f32[32,5120]{1,0:T(8,128)} async-done(((f32[128,5120]{1,0:T(8,128)}), f32[32,5120]{1,0:T(8,128)}) %reduce-scatter.35.cloned.1.call-update) | async-done | bytes 655376 | tf_op jit(solution)/shard_map/while/body/eval_jaxpr/reduce_scatter | solution.py:187
  633.5 49.1 %reduce-scatter.37.cloned.1.call-done = f32[32,5120]{1,0:T(8,128)} async-done(((f32[128,5120]{1,0:T(8,128)}), f32[32,5120]{1,0:T(8,128)}) %reduce-scatter.37.cloned.1.call-update) | async-done | bytes 655376 | tf_op jit(solution)/shard_map/while/body/eval_jaxpr/reduce_scatter | solution.py:124
  700.2 59.2 %reduce-scatter.35.cloned.1.call-done = f32[32,5120]{1,0:T(8,128)} async-done(((f32[128,5120]{1,0:T(8,128)}), f32[32,5120]{1,0:T(8,128)}) %reduce-scatter.35.cloned.1.call-update) | async-done | bytes 655376 | tf_op jit(solution)/shard_map/while/body/eval_jaxpr/reduce_scatter | solution.py:187
  816.6 49.1 %reduce-scatter.37.cloned.1.call-done = f32[32,5120]{1,0:T(8,128)} async-done(((f32[128,5120]{1,0:T(8,128)}), f32[32,5120]{1,0:T(8,128)}) %reduce-scatter.37.cloned.1.call-update) | async-done | bytes 655376 | tf_op jit(solution)/shard_map/while/body/eval_jaxpr/reduce_scatter | solution.py:124
  883.5 58.6 %reduce-scatter.35.cloned.1.call-done = f32[32,5120]{1,0:T(8,128)} async-done(((f32[128,5120]{1,0:T(8,128)}), f32[32,5120]{1,0:T(8,128)}) %reduce-scatter.35.cloned.1.call-update) | async-done | bytes 655376 | tf_op jit(solution)/shard_map/while/body/eval_jaxpr/reduce_scatter | solution.py:187
  999.5 49.1 %reduce-scatter.37.cloned.1.call-done = f32[32,5120]{1,0:T(8,128)} async-done(((f32[128,5120]{1,0:T(8,128)}), f32[32,5120]{1,0:T(8,128)}) %reduce-scatter.37.cloned.1.call-update) | async-done | bytes 655376 | tf_op jit(solution)/shard_map/while/body/eval_jaxpr/reduce_scatter | solution.py:124
  1066.4 58.6 %reduce-scatter.35.cloned.1.call-done = f32[32,5120]{1,0:T(8,128)} async-done(((f32[128,5120]{1,0:T(8,128)}), f32[32,5120]{1,0:T(8,128)}) %reduce-scatter.35.cloned.1.call-update) | async-done | bytes 655376 | tf_op jit(solution)/shard_map/while/body/eval_jaxpr/reduce_scatter | solution.py:187
  1182.5 49.1 %reduce-scatter.37.cloned.1.call-done = f32[32,5120]{1,0:T(8,128)} async-done(((f32[128,5120]{1,0:T(8,128)}), f32[32,5120]{1,0:T(8,128)}) %reduce-scatter.37.cloned.1.call-update) | async-done | bytes 655376 | tf_op jit(solution)/shard_map/while/body/eval_jaxpr/reduce_scatter | solution.py:124
  1249.4 58.6 %reduce-scatter.35.cloned.1.call-done = f32[32,5120]{1,0:T(8,128)} async-done(((f32[128,5120]{1,0:T(8,128)}), f32[32,5120]{1,0:T(8,128)}) %reduce-scatter.35.cloned.1.call-update) | async-done | bytes 655376 | tf_op jit(solution)/shard_map/while/body/eval_jaxpr/reduce_scatter | solution.py:187
  1365.4 49.1 %reduce-scatter.37.cloned.1.call-done = f32[32,5120]{1,0:T(8,128)} async-done(((f32[128,5120]{1,0:T(8,128)}), f32[32,5120]{1,0:T(8,128)}) %reduce-scatter.37.cloned.1.call-update) | async-done | bytes 655376 | tf_op jit(solution)/shard_map/while/body/eval_jaxpr/reduce_scatter | solution.py:124
  1432.1 59.2 %reduce-scatter.35.cloned.1.call-done = f32[32,5120]{1,0:T(8,128)} async-done(((f32[128,5120]{1,0:T(8,128)}), f32[32,5120]{1,0:T(8,128)}) %reduce-scatter.35.cloned.1.call-update) | async-done | bytes 655376 | tf_op jit(solution)/shard_map/while/body/eval_jaxpr/reduce_scatter | solution.py:187
  1548.5 49.1 %reduce-scatter.37.cloned.1.call-done = f32[32,5120]{1,0:T(8,128)} async-done(((f32[128,5120]{1,0:T(8,128)}), f32[32,5120]{1,0:T(8,128)}) %reduce-scatter.37.cloned.1.call-update) | async-done | bytes 655376 | tf_op jit(solution)/shard_map/while/body/eval_jaxpr/reduce_scatter | solution.py:124
  1615.4 58.7 %reduce-scatter.35.cloned.1.call-done = f32[32,5120]{1,0:T(8,128)} async-done(((f32[128,5120]{1,0:T(8,128)}), f32[32,5120]{1,0:T(8,128)}) %reduce-scatter.35.cloned.1.call-update) | async-done | bytes 655376 | tf_op jit(solution)/shard_map/while/body/eval_jaxpr/reduce_scatter | solution.py:187
  1731.5 49.1 %reduce-scatter.37.cloned.1.call-done = f32[32,5120]{1,0:T(8,128)} async-done(((f32[128,5120]{1,0:T(8,128)}), f32[32,5120]{1,0:T(8,128)}) %reduce-scatter.37.cloned.1.call-update) | async-done | bytes 655376 | tf_op jit(solution)/shard_map/while/body/eval_jaxpr/reduce_scatter | solution.py:124
  1798.4 58.6 %reduce-scatter.35.cloned.1.call-done = f32[32,5120]{1,0:T(8,128)} async-done(((f32[128,5120]{1,0:T(8,128)}), f32[32,5120]{1,0:T(8,128)}) %reduce-scatter.35.cloned.1.call-update) | async-done | bytes 655376 | tf_op jit(solution)/shard_map/while/body/eval_jaxpr/reduce_scatter | solution.py:187
  1914.4 49.1 %reduce-scatter.37.cloned.1.call-done = f32[32,5120]{1,0:T(8,128)} async-done(((f32[128,5120]{1,0:T(8,128)}), f32[32,5120]{1,0:T(8,128)}) %reduce-scatter.37.cloned.1.call-update) | async-done | bytes 655376 | tf_op jit(solution)/shard_map/while/body/eval_jaxpr/reduce_scatter | solution.py:124
  1981.3 58.6 %reduce-scatter.35.cloned.1.call-done = f32[32,5120]{1,0:T(8,128)} async-done(((f32[128,5120]{1,0:T(8,128)}), f32[32,5120]{1,0:T(8,128)}) %reduce-scatter.35.cloned.1.call-update) | async-done | bytes 655376 | tf_op jit(solution)/shard_map/while/body/eval_jaxpr/reduce_scatter | solution.py:187
  2097.4 49.1 %reduce-scatter.37.cloned.1.call-done = f32[32,5120]{1,0:T(8,128)} async-done(((f32[128,5120]{1,0:T(8,128)}), f32[32,5120]{1,0:T(8,128)}) %reduce-scatter.37.cloned.1.call-update) | async-done | bytes 655376 | tf_op jit(solution)/shard_map/while/body/eval_jaxpr/reduce_scatter | solution.py:124
  2164.2 58.6 %reduce-scatter.35.cloned.1.call-done = f32[32,5120]{1,0:T(8,128)} async-done(((f32[128,5120]{1,0:T(8,128)}), f32[32,5120]{1,0:T(8,128)}) %reduce-scatter.35.cloned.1.call-update) | async-done | bytes 655376 | tf_op jit(solution)/shard_map/while/body/eval_jaxpr/reduce_scatter | solution.py:187
  2280.3 49.1 %reduce-scatter.37.cloned.1.call-done = f32[32,5120]{1,0:T(8,128)} async-done(((f32[128,5120]{1,0:T(8,128)}), f32[32,5120]{1,0:T(8,128)}) %reduce-scatter.37.cloned.1.call-update) | async-done | bytes 655376 | tf_op jit(solution)/shard_map/while/body/eval_jaxpr/reduce_scatter | solution.py:124
  2347.2 58.6 %reduce-scatter.35.cloned.1.call-done = f32[32,5120]{1,0:T(8,128)} async-done(((f32[128,5120]{1,0:T(8,128)}), f32[32,5120]{1,0:T(8,128)}) %reduce-scatter.35.cloned.1.call-update) | async-done | bytes 655376 | tf_op jit(solution)/shard_map/while/body/eval_jaxpr/reduce_scatter | solution.py:187
  2463.3 49.1 %reduce-scatter.37.cloned.1.call-done = f32[32,5120]{1,0:T(8,128)} async-done(((f32[128,5120]{1,0:T(8,128)}), f32[32,5120]{1,0:T(8,128)}) %reduce-scatter.37.cloned.1.call-update) | async-done | bytes 655376 | tf_op jit(solution)/shard_map/while/body/eval_jaxpr/reduce_scatter | solution.py:124
  2530.1 58.6 %reduce-scatter.35.cloned.1.call-done = f32[32,5120]{1,0:T(8,128)} async-done(((f32[128,5120]{1,0:T(8,128)}), f32[32,5120]{1,0:T(8,128)}) %reduce-scatter.35.cloned.1.call-update) | async-done | bytes 655376 | tf_op jit(solution)/shard_map/while/body/eval_jaxpr/reduce_scatter | solution.py:187
  2640.4 1269.5 %while.82 = (s32[]{:T(128)}, bf16[12,128,160]{1,2,0:T(8,128)(2,1)}, s32[12]{0:T(128)S(1)}, bf16[1536,160]{1,0:T(8,128)(2,1)}, bf16[160,5120]{1,0:T(8,128)(2,1)},...) while((s32[]{:T(128)}, bf16[12,128,160]{1,2,0:T(8,128)(2,1)}, ...), condition=%wide.region_15.16_spmd, body=%wide.region_13.15_spmd.sunk | while | flops 443023360 | bytes 36848008 | solution.py:177
  2646.4 51.3 %reduce-scatter.33.cloned.1.call-done = f32[32,5120]{1,0:T(8,128)} async-done(((f32[128,5120]{1,0:T(8,128)}), f32[32,5120]{1,0:T(8,128)}) %reduce-scatter.33.cloned.1.call-update) | async-done | bytes 655376 | tf_op jit(solution)/shard_map/while/body/eval_jaxpr/reduce_scatter | solution.py:124
  2751.3 52.3 %reduce-scatter.33.cloned.1.call-done = f32[32,5120]{1,0:T(8,128)} async-done(((f32[128,5120]{1,0:T(8,128)}), f32[32,5120]{1,0:T(8,128)}) %reduce-scatter.33.cloned.1.call-update) | async-done | bytes 655376 | tf_op jit(solution)/shard_map/while/body/eval_jaxpr/reduce_scatter | solution.py:124
  2857.2 52.3 %reduce-scatter.33.cloned.1.call-done = f32[32,5120]{1,0:T(8,128)} async-done(((f32[128,5120]{1,0:T(8,128)}), f32[32,5120]{1,0:T(8,128)}) %reduce-scatter.33.cloned.1.call-update) | async-done | bytes 655376 | tf_op jit(solution)/shard_map/while/body/eval_jaxpr/reduce_scatter | solution.py:124
  2963.1 52.2 %reduce-scatter.33.cloned.1.call-done = f32[32,5120]{1,0:T(8,128)} async-done(((f32[128,5120]{1,0:T(8,128)}), f32[32,5120]{1,0:T(8,128)}) %reduce-scatter.33.cloned.1.call-update) | async-done | bytes 655376 | tf_op jit(solution)/shard_map/while/body/eval_jaxpr/reduce_scatter | solution.py:124
  3068.9 52.3 %reduce-scatter.33.cloned.1.call-done = f32[32,5120]{1,0:T(8,128)} async-done(((f32[128,5120]{1,0:T(8,128)}), f32[32,5120]{1,0:T(8,128)}) %reduce-scatter.33.cloned.1.call-update) | async-done | bytes 655376 | tf_op jit(solution)/shard_map/while/body/eval_jaxpr/reduce_scatter | solution.py:124
  3174.7 52.3 %reduce-scatter.33.cloned.1.call-done = f32[32,5120]{1,0:T(8,128)} async-done(((f32[128,5120]{1,0:T(8,128)}), f32[32,5120]{1,0:T(8,128)}) %reduce-scatter.33.cloned.1.call-update) | async-done | bytes 655376 | tf_op jit(solution)/shard_map/while/body/eval_jaxpr/reduce_scatter | solution.py:124
  3280.6 52.3 %reduce-scatter.33.cloned.1.call-done = f32[32,5120]{1,0:T(8,128)} async-done(((f32[128,5120]{1,0:T(8,128)}), f32[32,5120]{1,0:T(8,128)}) %reduce-scatter.33.cloned.1.call-update) | async-done | bytes 655376 | tf_op jit(solution)/shard_map/while/body/eval_jaxpr/reduce_scatter | solution.py:124
  3386.5 52.3 %reduce-scatter.33.cloned.1.call-done = f32[32,5120]{1,0:T(8,128)} async-done(((f32[128,5120]{1,0:T(8,128)}), f32[32,5120]{1,0:T(8,128)}) %reduce-scatter.33.cloned.1.call-update) | async-done | bytes 655376 | tf_op jit(solution)/shard_map/while/body/eval_jaxpr/reduce_scatter | solution.py:124
  3492.4 52.3 %reduce-scatter.33.cloned.1.call-done = f32[32,5120]{1,0:T(8,128)} async-done(((f32[128,5120]{1,0:T(8,128)}), f32[32,5120]{1,0:T(8,128)}) %reduce-scatter.33.cloned.1.call-update) | async-done | bytes 655376 | tf_op jit(solution)/shard_map/while/body/eval_jaxpr/reduce_scatter | solution.py:124
  3598.3 52.3 %reduce-scatter.33.cloned.1.call-done = f32[32,5120]{1,0:T(8,128)} async-done(((f32[128,5120]{1,0:T(8,128)}), f32[32,5120]{1,0:T(8,128)}) %reduce-scatter.33.cloned.1.call-update) | async-done | bytes 655376 | tf_op jit(solution)/shard_map/while/body/eval_jaxpr/reduce_scatter | solution.py:124
  3704.2 52.3 %reduce-scatter.33.cloned.1.call-done = f32[32,5120]{1,0:T(8,128)} async-done(((f32[128,5120]{1,0:T(8,128)}), f32[32,5120]{1,0:T(8,128)}) %reduce-scatter.33.cloned.1.call-update) | async-done | bytes 655376 | tf_op jit(solution)/shard_map/while/body/eval_jaxpr/reduce_scatter | solution.py:124
  3810.1 52.3 %reduce-scatter.33.cloned.1.call-done = f32[32,5120]{1,0:T(8,128)} async-done(((f32[128,5120]{1,0:T(8,128)}), f32[32,5120]{1,0:T(8,128)}) %reduce-scatter.33.cloned.1.call-update) | async-done | bytes 655376 | tf_op jit(solution)/shard_map/while/body/eval_jaxpr/reduce_scatter | solution.py:124
  3915.4 73.2 %all-gather.15.cloned.1.call-done = f32[1536,640]{0,1:T(8,128)} async-done(((f32[1536,160]{0,1:T(8,128)}), f32[1536,640]{0,1:T(8,128)}) %all-gather.15.cloned.1.call-update) | async-done | bytes 3932176 | tf_op jit(solution)/shard_map/all_gather | solution.py:209
  4044.4 318.3 %while.86 = (s32[]{:T(128)}, bf16[5,1536,32]{2,1,0:T(8,128)(2,1)}, bf16[5,1536,32]{1,2,0:T(8,128)(2,1)}, bf16[5,1536,32]{1,2,0:T(8,128)(2,1)}, s32[5]{0:T(128)},...) while((s32[]{:T(128)}, bf16[5,1536,32]{2,1,0:T(8,128)(2,1)}, ...), condition=%wide.region_26.27_spmd.clone, body=%wide.region_22.26_spmd.clone.sunk | while | flops 259784208 | bytes 27660404 | solution.py:114
  4119.9 48.2 %while.89 = (s32[]{:T(128)}, f32[1536,32]{0,1:T(8,128)}, f32[1536,32]{0,1:T(8,128)}, bf16[3,512,32]{1,2,0:T(8,128)(2,1)}, s32[3]{0:T(128)}, /*index=5*/s32[1536]...) while((s32[]{:T(128)}, f32[1536,32]{0,1:T(8,128)}, ...), condition=%wide.region_25.25_spmd.clone, body=%wide.region_23.24_spmd.clone.sunk | while | flops 259784192 | bytes 25385684 | solution.py:111
  4183.5 48.2 %while.89 = (s32[]{:T(128)}, f32[1536,32]{0,1:T(8,128)}, f32[1536,32]{0,1:T(8,128)}, bf16[3,512,32]{1,2,0:T(8,128)(2,1)}, s32[3]{0:T(128)}, /*index=5*/s32[1536]...) while((s32[]{:T(128)}, f32[1536,32]{0,1:T(8,128)}, ...), condition=%wide.region_25.25_spmd.clone, body=%wide.region_23.24_spmd.clone.sunk | while | flops 259784192 | bytes 25385684 | solution.py:111
  4382.7 67.5 %all-reduce.2.cloned.1.call-done = bf16[1536,640]{0,1:T(8,128)(2,1)} async-done(((bf16[1536,640]{0,1:T(8,128)(2,1)}), bf16[1536,640]{0,1:T(8,128)(2,1)}) %all-reduce.2.cloned.1.call-update) | async-done | bytes 1966096 | tf_op jit(solution)/shard_map/psum | solution.py:228
  4603.0 49.5 %reduce-scatter.21.cloned.1.call-done = f32[160,640]{1,0:T(8,128)} async-done(((f32[160,5120]{1,0:T(8,128)}), f32[160,640]{1,0:T(8,128)}) %reduce-scatter.21.cloned.1.call-update) | async-done | bytes 409616 | tf_op jit(solution)/shard_map/reduce_scatter | solution.py:211
  4652.4 50.9 %reduce-scatter.23.cloned.1.call-done = f32[160,640]{1,0:T(8,128)} async-done(((f32[160,5120]{1,0:T(8,128)}), f32[160,640]{1,0:T(8,128)}) %reduce-scatter.23.cloned.1.call-update) | async-done | bytes 409616 | tf_op jit(solution)/shard_map/reduce_scatter | solution.py:212
  (1168 shorter events, 2544.8 us)
Async XLA Ops:
  7.2 300.6 %reduce-scatter.19.cloned.1.call-start = ((), (), s32[]{:S(2)}) async-start(), calls=%async_computation.10 | async-start | bytes 4915200 | tf_op jit(solution)/shard_map/reduce_scatter | solution.py:158
  234.7 152.7 %all-gather.7.cloned.1.call-start = ((), (), s32[]{:S(2)}) async-start(), calls=%async_computation.11 | async-start | bytes 4915200 | tf_op jit(solution)/shard_map/all_gather | solution.py:160
  310.4 103.5 %all-gather.11.cloned.1.call-start = ((), (), s32[]{:S(2)}) async-start(), calls=%async_computation.13 | async-start | bytes 1843200 | tf_op jit(solution)/shard_map/all_gather | solution.py:164
  311.1 130.5 %all-gather.9.cloned.1.call-start = ((), (), s32[]{:S(2)}) async-start(), calls=%async_computation.12 | async-start | bytes 1843200 | tf_op jit(solution)/shard_map/all_gather | solution.py:163
  448.4 128.7 %reduce-scatter.35.cloned.1.call-start = ((), (), s32[]{:S(2)}) async-start(), calls=%async_computation.24 | async-start | bytes 3276800 | tf_op jit(solution)/shard_map/while/body/eval_jaxpr/reduce_scatter | solution.py:187
  450.6 165.4 %all-gather.17.cloned.1.call-start = ((), (), s32[]{:S(2)}) async-start(), calls=%async_computation.26 | async-start | bytes 1638400 | tf_op jit(solution)/shard_map/while/body/eval_jaxpr/all_gather | solution.py:195
  518.4 60.9 %collective-permute-start.3 = (bf16[2,32,5120]{2,1,0:T(8,128)(2,1)S(1)}, bf16[2,32,5120]{2,1,0:T(8,128)(2,1)S(1)}, u32[]{:S(2)}, u32[]{:S(2)}) collective-permute-start(bf16[2,32,5120]{2,1,0:T(8,128)(2,1)S(1)} %pad_maximum_fusion.15), channel_id=1, source_target_pairs={{0,16},{8,24},{16,0},{24,8},{1,17},{9,25},{17,1},{25,9},{2,18},{10... | collective-permute-start | bytes 1966088 | tf_op jit(solution)/shard_map/while/body/eval_jaxpr/ppermute | solution.py:23
  631.3 128.1 %reduce-scatter.35.cloned.1.call-start = ((), (), s32[]{:S(2)}) async-start(), calls=%async_computation.24 | async-start | bytes 3276800 | tf_op jit(solution)/shard_map/while/body/eval_jaxpr/reduce_scatter | solution.py:187
  633.4 164.6 %all-gather.17.cloned.1.call-start = ((), (), s32[]{:S(2)}) async-start(), calls=%async_computation.26 | async-start | bytes 1638400 | tf_op jit(solution)/shard_map/while/body/eval_jaxpr/all_gather | solution.py:195
  700.1 61.3 %collective-permute-start.3 = (bf16[2,32,5120]{2,1,0:T(8,128)(2,1)S(1)}, bf16[2,32,5120]{2,1,0:T(8,128)(2,1)S(1)}, u32[]{:S(2)}, u32[]{:S(2)}) collective-permute-start(bf16[2,32,5120]{2,1,0:T(8,128)(2,1)S(1)} %pad_maximum_fusion.15), channel_id=1, source_target_pairs={{0,16},{8,24},{16,0},{24,8},{1,17},{9,25},{17,1},{25,9},{2,18},{10... | collective-permute-start | bytes 1966088 | tf_op jit(solution)/shard_map/while/body/eval_jaxpr/ppermute | solution.py:23
  814.4 127.6 %reduce-scatter.35.cloned.1.call-start = ((), (), s32[]{:S(2)}) async-start(), calls=%async_computation.24 | async-start | bytes 3276800 | tf_op jit(solution)/shard_map/while/body/eval_jaxpr/reduce_scatter | solution.py:187
  816.5 164.4 %all-gather.17.cloned.1.call-start = ((), (), s32[]{:S(2)}) async-start(), calls=%async_computation.26 | async-start | bytes 1638400 | tf_op jit(solution)/shard_map/while/body/eval_jaxpr/all_gather | solution.py:195
  883.4 60.8 %collective-permute-start.3 = (bf16[2,32,5120]{2,1,0:T(8,128)(2,1)S(1)}, bf16[2,32,5120]{2,1,0:T(8,128)(2,1)S(1)}, u32[]{:S(2)}, u32[]{:S(2)}) collective-permute-start(bf16[2,32,5120]{2,1,0:T(8,128)(2,1)S(1)} %pad_maximum_fusion.15), channel_id=1, source_target_pairs={{0,16},{8,24},{16,0},{24,8},{1,17},{9,25},{17,1},{25,9},{2,18},{10... | collective-permute-start | bytes 1966088 | tf_op jit(solution)/shard_map/while/body/eval_jaxpr/ppermute | solution.py:23
  997.4 127.6 %reduce-scatter.35.cloned.1.call-start = ((), (), s32[]{:S(2)}) async-start(), calls=%async_computation.24 | async-start | bytes 3276800 | tf_op jit(solution)/shard_map/while/body/eval_jaxpr/reduce_scatter | solution.py:187
  999.5 164.4 %all-gather.17.cloned.1.call-start = ((), (), s32[]{:S(2)}) async-start(), calls=%async_computation.26 | async-start | bytes 1638400 | tf_op jit(solution)/shard_map/while/body/eval_jaxpr/all_gather | solution.py:195
  1066.3 60.9 %collective-permute-start.3 = (bf16[2,32,5120]{2,1,0:T(8,128)(2,1)S(1)}, bf16[2,32,5120]{2,1,0:T(8,128)(2,1)S(1)}, u32[]{:S(2)}, u32[]{:S(2)}) collective-permute-start(bf16[2,32,5120]{2,1,0:T(8,128)(2,1)S(1)} %pad_maximum_fusion.15), channel_id=1, source_target_pairs={{0,16},{8,24},{16,0},{24,8},{1,17},{9,25},{17,1},{25,9},{2,18},{10... | collective-permute-start | bytes 1966088 | tf_op jit(solution)/shard_map/while/body/eval_jaxpr/ppermute | solution.py:23
  1180.3 127.7 %reduce-scatter.35.cloned.1.call-start = ((), (), s32[]{:S(2)}) async-start(), calls=%async_computation.24 | async-start | bytes 3276800 | tf_op jit(solution)/shard_map/while/body/eval_jaxpr/reduce_scatter | solution.py:187
  1182.4 164.4 %all-gather.17.cloned.1.call-start = ((), (), s32[]{:S(2)}) async-start(), calls=%async_computation.26 | async-start | bytes 1638400 | tf_op jit(solution)/shard_map/while/body/eval_jaxpr/all_gather | solution.py:195
  1249.3 60.8 %collective-permute-start.3 = (bf16[2,32,5120]{2,1,0:T(8,128)(2,1)S(1)}, bf16[2,32,5120]{2,1,0:T(8,128)(2,1)S(1)}, u32[]{:S(2)}, u32[]{:S(2)}) collective-permute-start(bf16[2,32,5120]{2,1,0:T(8,128)(2,1)S(1)} %pad_maximum_fusion.15), channel_id=1, source_target_pairs={{0,16},{8,24},{16,0},{24,8},{1,17},{9,25},{17,1},{25,9},{2,18},{10... | collective-permute-start | bytes 1966088 | tf_op jit(solution)/shard_map/while/body/eval_jaxpr/ppermute | solution.py:23
  1363.3 128.1 %reduce-scatter.35.cloned.1.call-start = ((), (), s32[]{:S(2)}) async-start(), calls=%async_computation.24 | async-start | bytes 3276800 | tf_op jit(solution)/shard_map/while/body/eval_jaxpr/reduce_scatter | solution.py:187
  1365.4 164.6 %all-gather.17.cloned.1.call-start = ((), (), s32[]{:S(2)}) async-start(), calls=%async_computation.26 | async-start | bytes 1638400 | tf_op jit(solution)/shard_map/while/body/eval_jaxpr/all_gather | solution.py:195
  1432.1 61.4 %collective-permute-start.3 = (bf16[2,32,5120]{2,1,0:T(8,128)(2,1)S(1)}, bf16[2,32,5120]{2,1,0:T(8,128)(2,1)S(1)}, u32[]{:S(2)}, u32[]{:S(2)}) collective-permute-start(bf16[2,32,5120]{2,1,0:T(8,128)(2,1)S(1)} %pad_maximum_fusion.15), channel_id=1, source_target_pairs={{0,16},{8,24},{16,0},{24,8},{1,17},{9,25},{17,1},{25,9},{2,18},{10... | collective-permute-start | bytes 1966088 | tf_op jit(solution)/shard_map/while/body/eval_jaxpr/ppermute | solution.py:23
  1546.4 127.7 %reduce-scatter.35.cloned.1.call-start = ((), (), s32[]{:S(2)}) async-start(), calls=%async_computation.24 | async-start | bytes 3276800 | tf_op jit(solution)/shard_map/while/body/eval_jaxpr/reduce_scatter | solution.py:187
  1548.5 164.4 %all-gather.17.cloned.1.call-start = ((), (), s32[]{:S(2)}) async-start(), calls=%async_computation.26 | async-start | bytes 1638400 | tf_op jit(solution)/shard_map/while/body/eval_jaxpr/all_gather | solution.py:195
  1615.3 60.8 %collective-permute-start.3 = (bf16[2,32,5120]{2,1,0:T(8,128)(2,1)S(1)}, bf16[2,32,5120]{2,1,0:T(8,128)(2,1)S(1)}, u32[]{:S(2)}, u32[]{:S(2)}) collective-permute-start(bf16[2,32,5120]{2,1,0:T(8,128)(2,1)S(1)} %pad_maximum_fusion.15), channel_id=1, source_target_pairs={{0,16},{8,24},{16,0},{24,8},{1,17},{9,25},{17,1},{25,9},{2,18},{10... | collective-permute-start | bytes 1966088 | tf_op jit(solution)/shard_map/while/body/eval_jaxpr/ppermute | solution.py:23
  1729.3 127.7 %reduce-scatter.35.cloned.1.call-start = ((), (), s32[]{:S(2)}) async-start(), calls=%async_computation.24 | async-start | bytes 3276800 | tf_op jit(solution)/shard_map/while/body/eval_jaxpr/reduce_scatter | solution.py:187
  1731.4 164.4 %all-gather.17.cloned.1.call-start = ((), (), s32[]{:S(2)}) async-start(), calls=%async_computation.26 | async-start | bytes 1638400 | tf_op jit(solution)/shard_map/while/body/eval_jaxpr/all_gather | solution.py:195
  1912.3 127.6 %reduce-scatter.35.cloned.1.call-start = ((), (), s32[]{:S(2)}) async-start(), calls=%async_computation.24 | async-start | bytes 3276800 | tf_op jit(solution)/shard_map/while/body/eval_jaxpr/reduce_scatter | solution.py:187
  1914.4 164.4 %all-gather.17.cloned.1.call-start = ((), (), s32[]{:S(2)}) async-start(), calls=%async_computation.26 | async-start | bytes 1638400 | tf_op jit(solution)/shard_map/while/body/eval_jaxpr/all_gather | solution.py:195
  1981.2 60.9 %collective-permute-start.3 = (bf16[2,32,5120]{2,1,0:T(8,128)(2,1)S(1)}, bf16[2,32,5120]{2,1,0:T(8,128)(2,1)S(1)}, u32[]{:S(2)}, u32[]{:S(2)}) collective-permute-start(bf16[2,32,5120]{2,1,0:T(8,128)(2,1)S(1)} %pad_maximum_fusion.15), channel_id=1, source_target_pairs={{0,16},{8,24},{16,0},{24,8},{1,17},{9,25},{17,1},{25,9},{2,18},{10... | collective-permute-start | bytes 1966088 | tf_op jit(solution)/shard_map/while/body/eval_jaxpr/ppermute | solution.py:23
  2095.2 127.6 %reduce-scatter.35.cloned.1.call-start = ((), (), s32[]{:S(2)}) async-start(), calls=%async_computation.24 | async-start | bytes 3276800 | tf_op jit(solution)/shard_map/while/body/eval_jaxpr/reduce_scatter | solution.py:187
  2097.3 164.4 %all-gather.17.cloned.1.call-start = ((), (), s32[]{:S(2)}) async-start(), calls=%async_computation.26 | async-start | bytes 1638400 | tf_op jit(solution)/shard_map/while/body/eval_jaxpr/all_gather | solution.py:195
  2164.2 60.8 %collective-permute-start.3 = (bf16[2,32,5120]{2,1,0:T(8,128)(2,1)S(1)}, bf16[2,32,5120]{2,1,0:T(8,128)(2,1)S(1)}, u32[]{:S(2)}, u32[]{:S(2)}) collective-permute-start(bf16[2,32,5120]{2,1,0:T(8,128)(2,1)S(1)} %pad_maximum_fusion.15), channel_id=1, source_target_pairs={{0,16},{8,24},{16,0},{24,8},{1,17},{9,25},{17,1},{25,9},{2,18},{10... | collective-permute-start | bytes 1966088 | tf_op jit(solution)/shard_map/while/body/eval_jaxpr/ppermute | solution.py:23
  2278.2 127.7 %reduce-scatter.35.cloned.1.call-start = ((), (), s32[]{:S(2)}) async-start(), calls=%async_computation.24 | async-start | bytes 3276800 | tf_op jit(solution)/shard_map/while/body/eval_jaxpr/reduce_scatter | solution.py:187
  2280.3 164.4 %all-gather.17.cloned.1.call-start = ((), (), s32[]{:S(2)}) async-start(), calls=%async_computation.26 | async-start | bytes 1638400 | tf_op jit(solution)/shard_map/while/body/eval_jaxpr/all_gather | solution.py:195
  2347.1 60.8 %collective-permute-start.3 = (bf16[2,32,5120]{2,1,0:T(8,128)(2,1)S(1)}, bf16[2,32,5120]{2,1,0:T(8,128)(2,1)S(1)}, u32[]{:S(2)}, u32[]{:S(2)}) collective-permute-start(bf16[2,32,5120]{2,1,0:T(8,128)(2,1)S(1)} %pad_maximum_fusion.15), channel_id=1, source_target_pairs={{0,16},{8,24},{16,0},{24,8},{1,17},{9,25},{17,1},{25,9},{2,18},{10... | collective-permute-start | bytes 1966088 | tf_op jit(solution)/shard_map/while/body/eval_jaxpr/ppermute | solution.py:23
  2461.1 127.6 %reduce-scatter.35.cloned.1.call-start = ((), (), s32[]{:S(2)}) async-start(), calls=%async_computation.24 | async-start | bytes 3276800 | tf_op jit(solution)/shard_map/while/body/eval_jaxpr/reduce_scatter | solution.py:187
  2463.2 164.4 %all-gather.17.cloned.1.call-start = ((), (), s32[]{:S(2)}) async-start(), calls=%async_computation.26 | async-start | bytes 1638400 | tf_op jit(solution)/shard_map/while/body/eval_jaxpr/all_gather | solution.py:195
  2530.1 60.8 %collective-permute-start.3 = (bf16[2,32,5120]{2,1,0:T(8,128)(2,1)S(1)}, bf16[2,32,5120]{2,1,0:T(8,128)(2,1)S(1)}, u32[]{:S(2)}, u32[]{:S(2)}) collective-permute-start(bf16[2,32,5120]{2,1,0:T(8,128)(2,1)S(1)} %pad_maximum_fusion.15), channel_id=1, source_target_pairs={{0,16},{8,24},{16,0},{24,8},{1,17},{9,25},{17,1},{25,9},{2,18},{10... | collective-permute-start | bytes 1966088 | tf_op jit(solution)/shard_map/while/body/eval_jaxpr/ppermute | solution.py:23
  3909.9 78.6 %all-gather.15.cloned.1.call-start = ((), (), s32[]{:S(2)}) async-start(), calls=%async_computation.15 | async-start | bytes 4915200 | tf_op jit(solution)/shard_map/all_gather | solution.py:209
  3910.5 121.8 %all-gather.13.cloned.1.call-start = ((), (), s32[]{:S(2)}) async-start(), calls=%async_computation.14 | async-start | bytes 2457600 | tf_op jit(solution)/shard_map/all_gather | solution.py:178
  3912.4 537.8 %all-reduce.2.cloned.1.call-start = ((), (), s32[]{:S(2)}) async-start(), calls=%async_computation.16 | async-start | bytes 3932160 | tf_op jit(solution)/shard_map/psum | solution.py:228
  4369.3 117.7 %reduce-scatter.31.cloned.1.call-start = ((), (), s32[]{:S(2)}) async-start(), calls=%async_computation.22 | async-start | bytes 737280
  4372.5 155.6 %reduce-scatter.29.cloned.1.call-start = ((), (), s32[]{:S(2)}) async-start(), calls=%async_computation.21 | async-start | bytes 1474560
  4382.6 182.3 %reduce-scatter.27.cloned.1.call-start = ((), (), s32[]{:S(2)}) async-start(), calls=%async_computation.20 | async-start | bytes 368640
  4457.3 144.2 %reduce-scatter.25.cloned.1.call-start = ((), (), s32[]{:S(2)}) async-start(), calls=%async_computation.19 | async-start | bytes 368640
  4458.3 194.1 %reduce-scatter.21.cloned.1.call-start = ((), (), s32[]{:S(2)}) async-start(), calls=%async_computation.17 | async-start | bytes 3686400 | tf_op jit(solution)/shard_map/reduce_scatter | solution.py:211
  4459.1 244.2 %reduce-scatter.23.cloned.1.call-start = ((), (), s32[]{:S(2)}) async-start(), calls=%async_computation.18 | async-start | bytes 3686400 | tf_op jit(solution)/shard_map/reduce_scatter | solution.py:212
  (175 other events, 4549.2 us)
Sparse Core Ops, SparseCore 0:
  234.8 72.9 reduce-scatter.18
  310.5 76.8 all-gather.6
  448.6 52.0 reduce-scatter.36
  502.9 74.2 reduce-scatter.34
  631.4 51.1 reduce-scatter.36
  684.9 74.4 reduce-scatter.34
  814.5 51.0 reduce-scatter.36
  867.8 74.1 reduce-scatter.34
  944.3 36.6 all-gather.16
  997.5 51.0 reduce-scatter.36
  1050.8 74.1 reduce-scatter.34
  1127.2 36.6 all-gather.16
  1180.4 51.0 reduce-scatter.36
  1233.7 74.2 reduce-scatter.34
  1363.4 51.0 reduce-scatter.36
  1416.8 74.4 reduce-scatter.34
  1546.5 51.0 reduce-scatter.36
  1599.8 74.2 reduce-scatter.34
  1729.4 51.0 reduce-scatter.36
  1782.7 74.2 reduce-scatter.34
  1912.4 51.0 reduce-scatter.36
  1965.7 74.1 reduce-scatter.34
  2042.1 36.6 all-gather.16
  2095.3 51.0 reduce-scatter.36
  2148.6 74.1 reduce-scatter.34
  2278.3 51.0 reduce-scatter.36
  2331.6 74.2 reduce-scatter.34
  2461.2 51.0 reduce-scatter.36
  2514.5 74.1 reduce-scatter.34
  2591.0 36.6 all-gather.16
  2646.6 51.0 reduce-scatter.32
  2751.4 52.1 reduce-scatter.32
  2857.3 52.0 reduce-scatter.32
  2963.2 52.0 reduce-scatter.32
  3069.0 52.1 reduce-scatter.32
  3174.9 52.1 reduce-scatter.32
  3280.8 52.1 reduce-scatter.32
  3386.6 52.1 reduce-scatter.32
  3492.5 52.1 reduce-scatter.32
  3598.4 52.1 reduce-scatter.32
  3704.3 52.1 reduce-scatter.32
  3810.2 52.1 reduce-scatter.32
  3912.0 76.4 all-gather.14
  3990.1 42.1 all-gather.12
  4369.4 80.7 all-reduce.1
  4490.8 37.3 reduce-scatter.28
  4605.5 46.8 reduce-scatter.20
  4656.4 46.8 reduce-scatter.22
  (13 shorter events, 443.0 us)
